TPU v7x, 32 devices: a whole 2x2x4 slice. The times are simulated.
32 devices in a mesh: ord: 8 (over y, x, core), ch: 4 (over z).
Axes of the slice: x: 2, y: 2, z: 4, core: 2. Of those that a mesh axis runs over, the one named last changes fastest.
Arguments:
- field_grid: bfloat16 [2, 64, 2, 352, 1440], P(None, 'ch', None, 'ord'), may hold values from -40 to 40
- norm_gain: float32 [64], P('ch'), may hold values from 0.1 to 1.9
- norm_bias: float32 [64], P('ch'), may hold values from -3 to 3
- order_table: int32 [512], replicated, may hold values from 0 to 511, as said below
- legendre: bfloat16 [512, 2, 352, 360], P(('ord', 'ch')), may hold values from -0.3125 to 0.3125
Outputs:
- coefficients: bfloat16 [512, 2, 2, 2, 64, 360], P(('ord', 'ch'))
Inputs may be any that keep to these rules, and one draw needn't show every extreme that they name: `order_table`: a permutation of the orders in which slots 2 q and 2 q + 1 hold orders p and 511 - p.
All inputs are finite; a program needn't handle non-finite values.
Results may differ from a plain program's by a relative error of at most 0.0062.
Values may be sent and summed in bfloat16 or wider, within the bound.
A program may use at most 128 MiB of HBM per device.

v0:
```python
from functools import partial
import math
import jax
import jax.numpy as jnp
from jax import lax
from jax.sharding import PartitionSpec as P


def slot_table(orders, length):
    sample = jnp.arange(length, dtype=jnp.int32)
    phases = sample[:, None] * orders[None, :] % length
    angles = phases.astype(jnp.float32) * (2.0 * math.pi / length)
    factor = 1.0 / math.sqrt(length)
    stacked = jnp.stack([jnp.cos(angles) * factor, -jnp.sin(angles) * factor], axis=2)
    return stacked.reshape(length, 2 * orders.shape[0]).astype(jnp.bfloat16)


def legendre_sums(arrived, legendre, orders):
    odd_order = orders % 2 == 1
    swapped = jnp.where(
        odd_order[:, None, None, None, None, None], arrived[:, :, :, :, ::-1], arrived
    )
    raw_sums = jnp.einsum(
        "srbcpi,spij->sprbcj", swapped, legendre, preferred_element_type=jnp.float32
    )
    half_degrees = legendre.shape[3]
    degree = (
        2 * jnp.arange(half_degrees, dtype=jnp.int32)[None, :]
        + jnp.arange(2, dtype=jnp.int32)[:, None]
    )
    allowed = degree[None, :, :] >= orders[:, None, None]
    return jnp.where(allowed[:, :, None, None, None, :], raw_sums, 0.0).astype(jnp.bfloat16)


def on_device(field_grid, norm_gain, norm_bias, order_table, legendre):
    batch_size, chan_local, hemis, cycle_local, longitudes = field_grid.shape
    order_total = order_table.shape[0]
    values = field_grid.astype(jnp.float32)
    cell_count = hemis * cycle_local * lax.axis_size("ord") * longitudes
    partial_sum = jnp.sum(values, axis=(2, 3, 4))
    totals, squares = lax.psum((partial_sum, jnp.sum(values * values, axis=(2, 3, 4))), "ord")
    average = totals / cell_count
    spread = squares / cell_count - average * average
    centered = values - average[:, :, None, None, None]
    inverse_scale = lax.rsqrt(spread + 1e-05) * norm_gain[None, :]
    normed = (
        centered * inverse_scale[:, :, None, None, None] + norm_bias[None, :, None, None, None]
    ).astype(jnp.bfloat16)
    twiddle = slot_table(order_table, longitudes)
    flat_rows = normed.reshape(-1, longitudes)
    fourier = lax.dot_general(
        twiddle, flat_rows, (((0,), (1,)), ((), ())), preferred_element_type=jnp.float32
    )
    fourier = fourier.reshape(order_total, 2, batch_size, chan_local, hemis, cycle_local)
    north = fourier[:, :, :, :, 0]
    south = fourier[:, :, :, :, 1]
    halves = jnp.stack([north + south, north - south], axis=4).astype(jnp.bfloat16)
    slot_count = legendre.shape[0]
    channel_groups = lax.axis_size("ch")
    first_slot = (lax.axis_index("ord") * channel_groups + lax.axis_index("ch")) * slot_count
    own_orders = lax.dynamic_slice_in_dim(order_table, first_slot, slot_count)
    transform = partial(legendre_sums, legendre=legendre, orders=own_orders)
    arrived = lax.all_to_all(
        lax.all_to_all(halves, "ord", split_axis=0, concat_axis=5, tiled=True),
        "ch",
        split_axis=0,
        concat_axis=3,
        tiled=True,
    )
    return transform(arrived)


def solution(mesh):
    placed = (
        P(None, "ch", None, "ord", None),
        P("ch"),
        P("ch"),
        P(),
        P(("ord", "ch"), None, None, None),
    )
    return jax.shard_map(
        on_device,
        mesh=mesh,
        in_specs=placed,
        out_specs=P(("ord", "ch"), None, None, None, None, None),
        check_vma=False,
    )
```

profile of v0, /device:TPU:0, one launch (start us, length us, event | category | flops | bytes accessed | tf_op | source)
XLA Modules:
  0.0 532.1 jit_solution(7866468105255323386)
XLA Ops:
  0.0 0.0 copy-start
  0.0 21.6 %convert_reduce_fusion = (f32[2,16]{1,0:T(2,128)S(1)}, f32[2,16]{1,0:T(2,128)S(1)}) fusion(bf16[2,16,2,44,1440]{4,2,3,1,0:T(2,128)(2,1)} %param.5), kind=kLoop, calls=%fused_computation.2 | loop fusion | flops 16220096 | bytes 8110336 | tf_op jit(solution)/shard_map/reduce_sum | solution.py:40
  21.6 0.0 copy-done
  21.6 12.8 %multiply_convert_fusion.1 = (bf16[1440,512,1]{1,0,2:T(8,128)(2,1)S(1)}, bf16[1440,512,1]{1,0,2:T(8,128)(2,1)S(1)}) fusion(s32[512]{0:T(512)S(1)} %copy-done), kind=kLoop, calls=%fused_computation.24 | loop fusion | flops 10321920 | bytes 2951168 | tf_op jit(solution)/shard_map/convert.2
  34.3 1.9 pad_maximum_fusion.1
  36.2 7.4 %copy.27 = bf16[1440,512,2]{0,2,1:T(2,128)(2,1)S(1)} copy(bf16[1440,512,2]{1,0,2:T(8,128)(2,1)} %pad_maximum_fusion.1) | data formatting | bytes 5898240 | tf_op jit(solution)/shard_map/stack | solution.py:14
  43.6 0.0 copy-start.2
  43.6 0.0 copy-start.1
  43.6 3.5 convert_element_type.29
  47.2 6.1 %dot_general.11 = bf16[512,2,1440]{2,1,0:T(2,128)(2,1)S(1)} reshape(bf16[1024,1440]{1,0:T(8,128)(2,1)} %bitcast.26) | data formatting | bytes 5898240 | tf_op jit(solution)/shard_map/dot_general | solution.py:51
  53.3 15.3 %all-reduce = (f32[2,16]{1,0:T(2,128)S(1)}, f32[2,16]{1,0:T(2,128)S(1)}) all-reduce(f32[2,16]{1,0:T(2,128)S(1)} %get-tuple-element.6, f32[2,16]{1,0:T(2,128)S(1)} %get-tuple-element.5), channel_id=1, replica_groups=mesh['ord'=8,'ch'=4] {'ord'}, use_global_device_ids=true, to_apply=%region_3.0 | all-reduce | flops 64 | bytes 512 | tf_op jit(solution)/shard_map/psum | solution.py:41
  68.7 0.0 copy-done.2
  68.7 0.0 copy-done.1
  68.7 14.5 %fusion.2 = bf16[2,16,2,44,1440]{4,2,3,1,0:T(2,128)(2,1)} fusion(bf16[2,16,2,44,1440]{4,2,3,1,0:T(2,128)(2,1)} %param.5, f32[16]{0:T(128)S(1)} %copy-done.1, f32[2,16]{1,0:T(2,128)S(1)} %get-tuple-element.16, f32[2,16]{1,0:T(2,128)S(1)} %get-tuple-element.15), kind=kLoop, calls=%fused_computation.5 | loop fusion | flops 20275200 | bytes 16220480 | tf_op jit(solution)/shard_map/convert_element_type | solution.py:48
  83.2 12.6 %fusion.4 = f32[512,2,2,16,2,44]{0,5,4,3,2,1:T(8,128)S(1)} fusion(bf16[2,16,2,44,1440]{4,2,3,1,0:T(2,128)(2,1)} %fusion.2, bf16[512,2,1440,1,1,1]{2,1,0,5,4,3:T(2,128)(2,1)S(1)} %bitcast.27), kind=kOutput, calls=%fused_computation.9 | convolution fusion | flops 8304721920 | bytes 22593536 | tf_op jit(solution)/shard_map/dot_general | solution.py:51
  95.8 2.3 add_convert_fusion
  98.1 3.3 pad_maximum_fusion
  101.4 40.4 %copy.30 = bf16[512,2,2,16,2,44]{5,4,3,2,1,0:T(2,128)(2,1)} copy(bf16[512,2,2,16,2,44]{0,5,4,3,2,1:T(8,128)(2,1)} %pad_maximum_fusion) | data formatting | bytes 11534336 | tf_op jit(solution)/shard_map/stack | solution.py:57
  141.8 46.0 %reshape.129 = bf16[8,2,180224]{2,1,0:T(2,128)(2,1)} reshape(bf16[512,2,2,16,2,44]{5,4,3,2,1,0:T(2,128)(2,1)} %copy.30) | data formatting | bytes 11534336
  187.9 71.0 %all_to_all.36 = bf16[8,2,180224]{2,1,0:T(2,128)(2,1)} all-to-all(bf16[8,2,180224]{2,1,0:T(2,128)(2,1)} %reshape.129), channel_id=1, replica_groups=mesh['ord'=8,'ch'=4] {'ord'}, dimensions={0} | all-to-all | bytes 11534336 | tf_op jit(solution)/shard_map/all_to_all | solution.py:64
  258.8 50.2 %reshape.130 = bf16[512,2,2,16,2,44]{5,4,3,2,1,0:T(2,128)(2,1)} reshape(bf16[8,2,180224]{2,1,0:T(2,128)(2,1)} %all_to_all.36) | data formatting | bytes 11534336
  309.0 44.8 %copy.41 = bf16[8,64,2,2,16,2,44]{1,4,6,0,5,3,2:T(8,128)(2,1)} copy(bf16[8,64,2,2,16,2,44]{6,5,4,3,2,1,0:T(2,128)(2,1)} %bitcast.23) | data formatting | bytes 11534336 | tf_op jit(solution)/shard_map/all_to_all | solution.py:64
  353.8 18.0 %copy.33 = bf16[64,2,2,16,2,352]{5,3,4,2,1,0:T(8,128)(2,1)} copy(bf16[64,2,2,16,2,352]{0,3,5,4,2,1:T(8,128)(2,1)} %bitcast.24) | data formatting | bytes 11534336 | tf_op jit(solution)/shard_map/all_to_all | solution.py:64
  371.8 5.5 %all-to-all-start.1 = ((bf16[64,2,2,16,2,352]{5,3,4,2,1,0:T(8,128)(2,1)}), bf16[64,2,2,16,2,352]{5,3,4,2,1,0:T(8,128)(2,1)}, u32[]{:S(2)}, u32[]{:S(2)}) async-start(bf16[64,2,2,16,2,352]{5,3,4,2,1,0:T(8,128)(2,1)} %copy.33), calls=%async_computation.1 | async-start | bytes 12582912 | tf_op jit(solution)/shard_map/all_to_all | solution.py:63
  377.4 0.1 fusion.20
  377.5 0.1 broadcast_compare_fusion
  377.6 137.6 %all-to-all-done.1 = bf16[64,2,2,16,2,352]{5,3,4,2,1,0:T(8,128)(2,1)} async-done(((bf16[64,2,2,16,2,352]{5,3,4,2,1,0:T(8,128)(2,1)}), bf16[64,2,2,16,2,352]{5,3,4,2,1,0:T(8,128)(2,1)}, u32[]{:S(2)}, u32[]{:S(2)}) %all-to-all-start.1) | async-done | bytes 5767200 | tf_op jit(solution)/shard_map/all_to_all | solution.py:63
  515.2 4.0 copy.34
  519.1 3.3 reverse_select_fusion
  522.4 9.7 %select_convert_fusion = bf16[16,2,2,2,64,360]{5,4,3,2,1,0:T(8,128)(2,1)} fusion(pred[16,2,360]{2,1,0:T(4,128)(4,1)S(1)} %broadcast_compare_fusion, bf16[16,2,352,360]{3,2,1,0:T(8,128)(2,1)} %param.9, bf16[16,2,2,64,2,352]{5,3,4,2,1,0:T(8,128)(2,1)S(1)} %reverse_select_fusion), kind=kOutput, calls=%fused_computation.7 | convolution fusion | flops 2082078720 | bytes 19787008 | tf_op jit(solution)/shard_map/srbcpi,spij->sprbcj/dot_general | solution.py:23
  (3 shorter events, 0.0 us)
Async XLA Ops:
  0.0 21.6 %copy-start = (s32[512]{0:T(512)S(1)}, s32[512]{0:T(512)}, u32[]{:S(2)}) copy-start(s32[512]{0:T(512)} %param.8) | copy-start | bytes 6148
  43.6 25.0 %copy-start.2 = (f32[16]{0:T(128)S(1)}, f32[16]{0:T(128)}, u32[]{:S(2)}) copy-start(f32[16]{0:T(128)} %param.6) | copy-start | bytes 196
  43.6 25.0 %copy-start.1 = (f32[16]{0:T(128)S(1)}, f32[16]{0:T(128)}, u32[]{:S(2)}) copy-start(f32[16]{0:T(128)} %param.7) | copy-start | bytes 196
  371.8 143.3 %all-to-all-start.1 = ((bf16[64,2,2,16,2,352]{5,3,4,2,1,0:T(8,128)(2,1)}), bf16[64,2,2,16,2,352]{5,3,4,2,1,0:T(8,128)(2,1)}, u32[]{:S(2)}, u32[]{:S(2)}) async-start(bf16[64,2,2,16,2,352]{5,3,4,2,1,0:T(8,128)(2,1)} %copy.33), calls=%async_computation.1 | async-start | bytes 12582912 | tf_op jit(solution)/shard_map/all_to_all | solution.py:63
where the time goes:
time: 536 us; the launch traced here: 532 us
  local copies, waits for them, and re-layouts  220 us (41%)
  waiting for transfers between devices  138 us (26%)
  blocking collectives  86.3 us (16%)
  other arithmetic  59.8 us (11%)
  matrix products  22.3 us (4%)
  starting transfers between devices  5.52 us (1%)
    all_to_all x1, waiting for transfers between devices, on_device(): lax.all_to_all(lax.all_to_all(halves, 'ord', split_axis=0, concat_axis=5,...  138 us
    unnamed x8, local copies, waits for them, and re-layouts  96.2 us
    all_to_all x1, blocking collectives, on_device(): lax.all_to_all(halves, 'ord', split_axis=0, concat_axis=5, tiled=True)  71 us
    all_to_all x2, local copies, waits for them, and re-layouts, on_device(): lax.all_to_all(halves, 'ord', split_axis=0, concat_axis=5, tiled=True)  62.8 us
    another operation x1, local copies, waits for them, and re-layouts, on_device(): jnp.stack([north + south, north - south], axis=4).astype(jnp.bfloat16)  40.4 us
    reduce_sum x1, other arithmetic, on_device(): partial_sum = jnp.sum(values, axis=(2, 3, 4))  21.6 us
    psum x1, blocking collectives, on_device(): lax.psum((partial_sum, jnp.sum(values * values, axis=(2, 3, 4))), 'ord')  15.3 us
    another operation x2, other arithmetic  15 us
  transfers between devices with their start and end apart: 1, of which 1 were waited for; matrix products, arithmetic and copies ran while one was open for 0% of the time, Pallas kernels for 0%

commit v1 on v0

--- a/solution.py
+++ b/solution.py
@@ -60,12 +60,20 @@
     first_slot = (lax.axis_index("ord") * channel_groups + lax.axis_index("ch")) * slot_count
     own_orders = lax.dynamic_slice_in_dim(order_table, first_slot, slot_count)
     transform = partial(legendre_sums, legendre=legendre, orders=own_orders)
-    arrived = lax.all_to_all(
-        lax.all_to_all(halves, "ord", split_axis=0, concat_axis=5, tiled=True),
-        "ch",
-        split_axis=0,
-        concat_axis=3,
-        tiled=True,
+    arrived = jnp.concatenate(
+        lax.all_to_all(
+            jnp.stack(
+                jnp.split(
+                    lax.all_to_all(halves, "ord", split_axis=0, concat_axis=5, tiled=True),
+                    lax.axis_size("ch"),
+                    axis=0,
+                )
+            ),
+            "ch",
+            0,
+            0,
+        ),
+        axis=3,
     )
     return transform(arrived)
 

time: 536 us -> 654 us (1.22)
  local copies, waits for them, and re-layouts: 220 us -> 327 us
    split x0 -> x5, local copies, waits for them, and re-layouts: none -> 102 us  [on_device(): jnp.split(lax.all_to_all(halves, 'ord', split_axis=0, concat_axis=5, tile...]
    another operation x0 -> x4, local copies, waits for them, and re-layouts: none -> 23.9 us  [on_device(): jnp.stack(jnp.split(lax.all_to_all(halves, 'ord', split_axis=0, concat_ax...]
    all_to_all x2 -> x1, local copies, waits for them, and re-layouts: 62.8 us -> 43.3 us  [on_device(): lax.all_to_all(halves, 'ord', split_axis=0, concat_axis=5, tiled=True)]
    another operation x2 -> x3, other arithmetic: 15 us -> 20.7 us
where the time goes in v1:
time: 654 us; the launch traced here: 645 us
  local copies, waits for them, and re-layouts  327 us (50%)
  waiting for transfers between devices  138 us (21%)
  blocking collectives  86.6 us (13%)
  other arithmetic  65.4 us (10%)
  matrix products  22.3 us (3%)
    all_to_all x1, waiting for transfers between devices, on_device(): lax.all_to_all(jnp.stack(jnp.split(lax.all_to_all(halves, 'ord', split_ax...  138 us
    split x5, local copies, waits for them, and re-layouts, on_device(): jnp.split(lax.all_to_all(halves, 'ord', split_axis=0, concat_axis=5, tile...  102 us
    unnamed x8, local copies, waits for them, and re-layouts  96.7 us
    all_to_all x1, blocking collectives, on_device(): lax.all_to_all(halves, 'ord', split_axis=0, concat_axis=5, tiled=True)  71.2 us
    all_to_all x1, local copies, waits for them, and re-layouts, on_device(): lax.all_to_all(halves, 'ord', split_axis=0, concat_axis=5, tiled=True)  43.3 us
    another operation x1, local copies, waits for them, and re-layouts, on_device(): jnp.stack([north + south, north - south], axis=4).astype(jnp.bfloat16)  40.3 us
    another operation x4, local copies, waits for them, and re-layouts, on_device(): jnp.stack(jnp.split(lax.all_to_all(halves, 'ord', split_axis=0, concat_ax...  23.9 us
    reduce_sum x1, other arithmetic, on_device(): partial_sum = jnp.sum(values, axis=(2, 3, 4))  21.6 us
  transfers between devices with their start and end apart: 1, of which 1 were waited for; matrix products, arithmetic and copies ran while one was open for 0% of the time, Pallas kernels for 0%

profile of v1, /device:TPU:0, one launch (start us, length us, event | category | flops | bytes accessed | tf_op | source)
XLA Modules:
  0.0 644.7 jit_solution(17531438197373314975)
XLA Ops:
  0.0 21.6 %convert_reduce_fusion = (f32[2,16]{1,0:T(2,128)S(1)}, f32[2,16]{1,0:T(2,128)S(1)}) fusion(bf16[2,16,2,44,1440]{4,2,3,1,0:T(2,128)(2,1)} %param.5), kind=kLoop, calls=%fused_computation.2 | loop fusion | flops 16220096 | bytes 8110336 | tf_op jit(solution)/shard_map/reduce_sum | solution.py:40
  21.6 12.8 %multiply_convert_fusion.1 = (bf16[1440,512,1]{1,0,2:T(8,128)(2,1)S(1)}, bf16[1440,512,1]{1,0,2:T(8,128)(2,1)S(1)}) fusion(s32[512]{0:T(512)S(1)} %copy-done), kind=kLoop, calls=%fused_computation.25 | loop fusion | flops 10321920 | bytes 2951168 | tf_op jit(solution)/shard_map/convert.2
  34.3 1.9 pad_maximum_fusion.2
  36.2 7.4 %copy.33 = bf16[1440,512,2]{0,2,1:T(2,128)(2,1)S(1)} copy(bf16[1440,512,2]{1,0,2:T(8,128)(2,1)} %pad_maximum_fusion.2) | data formatting | bytes 5898240 | tf_op jit(solution)/shard_map/stack | solution.py:14
  43.6 3.5 convert_element_type.29
  47.2 6.1 dot_general.11
  53.3 15.4 %all-reduce = (f32[2,16]{1,0:T(2,128)S(1)}, f32[2,16]{1,0:T(2,128)S(1)}) all-reduce(f32[2,16]{1,0:T(2,128)S(1)} %get-tuple-element.6, f32[2,16]{1,0:T(2,128)S(1)} %get-tuple-element.5), channel_id=1, replica_groups=mesh['ord'=8,'ch'=4] {'ord'}, use_global_device_ids=true, to_apply=%region_3.0 | all-reduce | flops 64 | bytes 512 | tf_op jit(solution)/shard_map/psum | solution.py:41
  68.8 14.5 %fusion.2 = bf16[2,16,2,44,1440]{4,2,3,1,0:T(2,128)(2,1)} fusion(bf16[2,16,2,44,1440]{4,2,3,1,0:T(2,128)(2,1)} %param.5, f32[16]{0:T(128)S(1)} %copy-done.1, f32[2,16]{1,0:T(2,128)S(1)} %get-tuple-element.20, f32[2,16]{1,0:T(2,128)S(1)} %get-tuple-element.19), kind=kLoop, calls=%fused_computation.5 | loop fusion | flops 20275200 | bytes 16220480 | tf_op jit(solution)/shard_map/convert_element_type | solution.py:48
  83.3 12.6 %fusion.4 = f32[512,2,2,16,2,44]{0,5,4,3,2,1:T(8,128)S(1)} fusion(bf16[2,16,2,44,1440]{4,2,3,1,0:T(2,128)(2,1)} %fusion.2, bf16[512,2,1440,1,1,1]{2,1,0,5,4,3:T(2,128)(2,1)S(1)} %bitcast.38), kind=kOutput, calls=%fused_computation.9 | convolution fusion | flops 8304721920 | bytes 22593536 | tf_op jit(solution)/shard_map/dot_general | solution.py:51
  95.9 2.3 add_convert_fusion
  98.2 3.3 pad_maximum_fusion
  101.5 40.3 %copy.36 = bf16[512,2,2,16,2,44]{5,4,3,2,1,0:T(2,128)(2,1)} copy(bf16[512,2,2,16,2,44]{0,5,4,3,2,1:T(8,128)(2,1)} %pad_maximum_fusion) | data formatting | bytes 11534336 | tf_op jit(solution)/shard_map/stack | solution.py:57
  141.9 46.5 %reshape.145 = bf16[8,2,180224]{2,1,0:T(2,128)(2,1)} reshape(bf16[512,2,2,16,2,44]{5,4,3,2,1,0:T(2,128)(2,1)} %copy.36) | data formatting | bytes 11534336
  188.4 71.2 %all_to_all.20 = bf16[8,2,180224]{2,1,0:T(2,128)(2,1)} all-to-all(bf16[8,2,180224]{2,1,0:T(2,128)(2,1)} %reshape.145), channel_id=1, replica_groups=mesh['ord'=8,'ch'=4] {'ord'}, dimensions={0} | all-to-all | bytes 11534336 | tf_op jit(solution)/shard_map/all_to_all | solution.py:67
  259.5 50.2 %reshape.146 = bf16[512,2,2,16,2,44]{5,4,3,2,1,0:T(2,128)(2,1)} reshape(bf16[8,2,180224]{2,1,0:T(2,128)(2,1)} %all_to_all.20) | data formatting | bytes 11534336
  309.7 43.3 %copy.48 = bf16[8,64,2,2,16,2,44]{1,0,4,6,5,3,2:T(8,128)(2,1)} copy(bf16[8,64,2,2,16,2,44]{6,5,4,3,2,1,0:T(2,128)(2,1)} %bitcast.35) | data formatting | bytes 11534336 | tf_op jit(solution)/shard_map/all_to_all | solution.py:67
  353.0 32.4 %fusion.22 = (bf16[16,2,2,16,2,8,44]{0,5,3,6,4,2,1:T(8,128)(2,1)}, bf16[16,2,2,16,2,8,44]{0,5,3,6,4,2,1:T(8,128)(2,1)}, bf16[16,2,2,16,2,8,44]{0,5,3,6,4,2,1:T(8,128)(2,1)}, bf16[16,2,2,16,2,8,44]{0,5,3,6,4,2,1:T(8,128)(2,1)}) fusion(bf16[64,2,2,16,2,8,44]{0,5,3,6,4,2,1:T(8,128)(2,1)} %bitcast.34), kind=kLoop, calls=%fused_computation.40 | loop fusion | bytes 11534336 | tf_op jit(solution)/shard_map/split | solution.py:66
  385.4 17.3 %copy.38 = bf16[16,2,2,16,2,8,44]{6,5,3,4,2,1,0:T(8,128)(2,1)} copy(bf16[16,2,2,16,2,8,44]{0,5,3,6,4,2,1:T(8,128)(2,1)} %get-tuple-element.13) | data formatting | bytes 2883584 | tf_op jit(solution)/shard_map/split | solution.py:66
  402.7 5.5 stack.29
  408.3 17.3 %copy.39 = bf16[16,2,2,16,2,8,44]{6,5,3,4,2,1,0:T(8,128)(2,1)} copy(bf16[16,2,2,16,2,8,44]{0,5,3,6,4,2,1:T(8,128)(2,1)} %get-tuple-element.16) | data formatting | bytes 2883584 | tf_op jit(solution)/shard_map/split | solution.py:66
  425.6 5.5 stack.30
  431.1 17.3 %copy.40 = bf16[16,2,2,16,2,8,44]{6,5,3,4,2,1,0:T(8,128)(2,1)} copy(bf16[16,2,2,16,2,8,44]{0,5,3,6,4,2,1:T(8,128)(2,1)} %get-tuple-element.15) | data formatting | bytes 2883584 | tf_op jit(solution)/shard_map/split | solution.py:66
  448.4 6.4 stack.31
  454.8 17.5 %copy.41 = bf16[16,2,2,16,2,8,44]{6,5,3,4,2,1,0:T(8,128)(2,1)} copy(bf16[16,2,2,16,2,8,44]{0,5,3,6,4,2,1:T(8,128)(2,1)} %get-tuple-element.14) | data formatting | bytes 2883584 | tf_op jit(solution)/shard_map/split | solution.py:66
  472.3 6.4 stack.32
  478.7 5.6 pad_maximum_fusion.1
  484.4 5.3 all-to-all-start.1
  489.7 0.1 broadcast_compare_fusion
  489.8 137.6 %all-to-all-done.1 = bf16[4,16,2,2,16,2,352]{6,4,5,3,2,1,0:T(8,128)(2,1)} async-done(((bf16[4,16,2,2,16,2,352]{6,4,5,3,2,1,0:T(8,128)(2,1)}), bf16[4,16,2,2,16,2,352]{6,4,5,3,2,1,0:T(8,128)(2,1)}, u32[]{:S(2)}, u32[]{:S(2)}) %all-to-all-start.1) | async-done | bytes 5767200 | tf_op jit(solution)/shard_map/all_to_all | solution.py:64
  627.5 4.0 copy.42
  631.4 3.3 reverse_select_fusion
  634.7 9.7 %select_convert_fusion = bf16[16,2,2,2,64,360]{5,4,3,2,1,0:T(8,128)(2,1)} fusion(pred[16,2,360]{2,1,0:T(4,128)(4,1)S(1)} %broadcast_compare_fusion, bf16[16,2,352,360]{3,2,1,0:T(8,128)(2,1)} %param.9, bf16[16,2,2,64,2,352]{5,3,4,2,1,0:T(8,128)(2,1)S(1)} %reverse_select_fusion), kind=kOutput, calls=%fused_computation.7 | convolution fusion | flops 2082078720 | bytes 19787008 | tf_op jit(solution)/shard_map/srbcpi,spij->sprbcj/dot_general | solution.py:23
  (10 shorter events, 0.1 us)
Async XLA Ops:
  0.0 21.6 %copy-start = (s32[512]{0:T(512)S(1)}, s32[512]{0:T(512)}, u32[]{:S(2)}) copy-start(s32[512]{0:T(512)} %param.8) | copy-start | bytes 6148
  43.6 25.1 %copy-start.2 = (f32[16]{0:T(128)S(1)}, f32[16]{0:T(128)}, u32[]{:S(2)}) copy-start(f32[16]{0:T(128)} %param.6) | copy-start | bytes 196
  43.6 25.1 %copy-start.1 = (f32[16]{0:T(128)S(1)}, f32[16]{0:T(128)}, u32[]{:S(2)}) copy-start(f32[16]{0:T(128)} %param.7) | copy-start | bytes 196
  484.4 143.1 %all-to-all-start.1 = ((bf16[4,16,2,2,16,2,352]{6,4,5,3,2,1,0:T(8,128)(2,1)}), bf16[4,16,2,2,16,2,352]{6,4,5,3,2,1,0:T(8,128)(2,1)}, u32[]{:S(2)}, u32[]{:S(2)}) async-start(bf16[4,16,2,2,16,2,352]{6,4,5,3,2,1,0:T(8,128)(2,1)} %pad_maximum_fusion.1), calls=%async_computation.1 | async-start | bytes 12582912 | tf_op jit(solution)/shard_map/all_to_all | solution.py:64
